TPU v7x, 32 devices: a whole 2x2x4 slice. The times are simulated.
32 devices in a mesh: tile: 4 (over y, x), slab: 8 (over z, core).
Axes of the slice: x: 2, y: 2, z: 4, core: 2. Of those that a mesh axis runs over, the one named last changes fastest.
Arguments:
- raw_stack: bfloat16 [32, 120, 2048], P('slab', None, 'tile'), may hold values from -48 to 48
- shear_offsets: int32 [32], P('slab'), may hold values from 0 to 8
- intersection_widths: int32 [3], replicated, may hold values from 32 to 128
Outputs:
- difference: bfloat16 [128, 32, 2048], P('slab', None, 'tile')
- level_one: bfloat16 [64, 16, 1024], P('slab', None, 'tile')
- level_two: bfloat16 [32, 8, 512], P('slab', None, 'tile')
All inputs are finite; a program needn't handle non-finite values.
Results may differ from a plain program's by a relative error of at most 0.003.
Values may be sent and summed in bfloat16 or wider, within the bound.
No kernel may reach another device: no remote copies, remote signals or barrier semaphores. Data moves between devices by JAX's collectives and lax.ppermute only.
A program may use at most 64 MiB of HBM per device.

v0:
```python
import math
import jax
import jax.numpy as jnp
from jax import lax
from jax.sharding import PartitionSpec as P

SLAB_ROWS = 16
STRIP = 6
RADIUS = 4


def padded_2(block, sides, width):
    for axis, dim in sides:
        count = lax.axis_size(axis)
        forward = [(i, i + 1) for i in range(count - 1)]
        backward = [(target, source) for source, target in forward]
        low = lax.ppermute(
            lax.slice_in_dim(block, block.shape[dim] - width, None, axis=dim), axis, forward
        )
        high = lax.ppermute(lax.slice_in_dim(block, 0, width, axis=dim), axis, backward)
        block = jnp.concatenate([low, block, high], axis=dim)
    return block


def shifted(block, axis, distance):
    devices = range(lax.axis_size(axis))
    route = [(i - distance, i) for i in devices if i - distance in devices]
    return lax.ppermute(block, axis, route)


def gauss_taps(sigma_value, reach_cells):
    entries = [
        math.exp(-(offset * offset) / (2.0 * sigma_value * sigma_value))
        for offset in range(-reach_cells, reach_cells + 1)
    ]
    weight_sum = sum(entries)
    return [entry_value / weight_sum for entry_value in entries]


def binomial_taps():
    return [1.0 / 16.0, 4.0 / 16.0, 6.0 / 16.0, 4.0 / 16.0, 1.0 / 16.0]


def smooth(source, weights, direction, begin_at, length_out, stride):
    result = weights[0] * lax.slice_in_dim(
        source, begin_at, begin_at + (length_out - 1) * stride + 1, stride, direction
    )
    for offset in range(1, len(weights)):
        lowest = begin_at + offset
        window = lax.slice_in_dim(
            source, lowest, lowest + (length_out - 1) * stride + 1, stride, direction
        )
        result = result + weights[offset] * window
    return result


def pad_scans(source, width_cells):
    return jnp.pad(source, ((0, 0), (width_cells, width_cells), (0, 0)))


def deskew(planes_block, shifts, shear_top, total_rows, margin):
    padded = jnp.pad(planes_block, ((0, 0), (shear_top + margin, shear_top + margin), (0, 0)))

    def place_plane(plane, shift_value):
        return lax.dynamic_slice_in_dim(plane, shear_top - shift_value, total_rows + 2 * margin, 0)

    return jax.vmap(place_plane, out_axes=1)(padded, shifts)


def band_table(weights, source_pos, target_pos):
    reach_cells = len(weights) // 2
    offsets = source_pos[:, None] - target_pos[None, :] + reach_cells
    table = jnp.zeros(offsets.shape, jnp.float32)
    for index_tap in range(len(weights)):
        table = table + weights[index_tap] * (offsets == index_tap).astype(jnp.float32)
    return table


def along_columns(pieces, tables):
    total = None
    for piece_field, table in zip(pieces, tables):
        term = jnp.einsum("rsc,co->rso", piece_field, table, precision=lax.Precision.HIGHEST)
        total = term if total is None else total + term
    return total


def body(raw_stack, shear_offsets, intersection_widths):
    slab_count = lax.axis_size("slab")
    tile_count = lax.axis_size("tile")
    tile_index = lax.axis_index("tile")
    planes, camera, columns = raw_stack.shape
    total_rows = SLAB_ROWS * slab_count
    shear_top = total_rows - camera
    row_depth = RADIUS
    deskewed = deskew(raw_stack, shear_offsets, shear_top, total_rows, 0)
    outgoing = deskewed.reshape(slab_count, SLAB_ROWS, planes, columns)
    volume = lax.all_to_all(outgoing, "slab", split_axis=0, concat_axis=2, tiled=True)[0]
    volume = padded_2(volume, (("slab", 0),), row_depth)
    right_width = intersection_widths[jnp.minimum(tile_index, tile_count - 2)]
    left_width = intersection_widths[jnp.maximum(tile_index - 1, 0)]
    toward_right = lax.dynamic_slice_in_dim(volume, columns - right_width - STRIP, STRIP, 2)
    toward_left = lax.dynamic_slice_in_dim(volume, left_width, STRIP, 2)
    from_left = shifted(toward_right, "tile", 1)
    from_right = shifted(toward_left, "tile", -1)
    pieces = (
        volume.astype(jnp.float32),
        from_left.astype(jnp.float32),
        from_right.astype(jnp.float32),
    )
    own_pos = jnp.arange(columns, dtype=jnp.int32)
    left_pos = jnp.arange(STRIP, dtype=jnp.int32) - STRIP
    right_pos = jnp.arange(STRIP, dtype=jnp.int32) + columns
    sources = (own_pos, left_pos, right_pos)
    scan_count = volume.shape[1]

    def gaussian(sigma_value):
        weights = gauss_taps(sigma_value, RADIUS)
        colled = along_columns(pieces, [band_table(weights, place, own_pos) for place in sources])
        along_rows = smooth(colled, weights, 0, row_depth - RADIUS, SLAB_ROWS, 1)
        return smooth(pad_scans(along_rows, RADIUS), weights, 1, 0, scan_count, 1)

    difference = (gaussian(1.0) - gaussian(1.6)).astype(jnp.bfloat16)
    binomial = binomial_taps()
    main_pos = 2 * jnp.arange(columns // 2, dtype=jnp.int32)
    edge_pos = jnp.array([-4, -2, columns, columns + 2], dtype=jnp.int32)
    target_pos = jnp.concatenate([main_pos, edge_pos])
    colled = along_columns(pieces, [band_table(binomial, place, target_pos) for place in sources])
    row_keep = jnp.ones((SLAB_ROWS // 2,), dtype=bool)
    coarse_count = SLAB_ROWS // 2
    rows_blur = smooth(colled, binomial, 0, row_depth - 2, coarse_count, 2)
    scans_blur = smooth(pad_scans(rows_blur, 2), binomial, 1, 0, scan_count // 2, 2)
    edge_keep = ((edge_pos >= 0) | (tile_index > 0)) & (
        (edge_pos < columns) | (tile_index < tile_count - 1)
    )
    main_ext = jnp.where(row_keep[:, None, None], scans_blur[:, :, 0 : columns // 2], 0.0).astype(
        jnp.bfloat16
    )
    edge_mask = row_keep[:, None, None] & edge_keep[None, None, :]
    edge_ext = jnp.where(edge_mask, scans_blur[:, :, columns // 2 :], 0.0).astype(jnp.bfloat16)
    main_index = jnp.arange(columns // 2, dtype=jnp.int32) + 2
    edge_index = jnp.array([0, 1, columns // 2 + 2, columns // 2 + 3], dtype=jnp.int32)
    coarse_target = 2 * jnp.arange(columns // 4, dtype=jnp.int32) + 2
    coarse_cols = along_columns(
        (main_ext.astype(jnp.float32), edge_ext.astype(jnp.float32)),
        [
            band_table(binomial, main_index, coarse_target),
            band_table(binomial, edge_index, coarse_target),
        ],
    )
    coarse_cols = padded_2(coarse_cols, (("slab", 0),), 2)
    rows_two = smooth(coarse_cols, binomial, 0, 0, SLAB_ROWS // 4, 2)
    level_two = smooth(pad_scans(rows_two, 2), binomial, 1, 0, scan_count // 4, 2).astype(
        jnp.bfloat16
    )
    return (difference, main_ext, level_two)


def solution(mesh):
    placed = (P("slab", None, "tile"), P("slab"), P())
    return jax.shard_map(
        body,
        mesh=mesh,
        in_specs=placed,
        out_specs=(P("slab", None, "tile"), P("slab", None, "tile"), P("slab", None, "tile")),
        check_vma=False,
    )
```

profile of v0, /device:TPU:1, one launch (start us, length us, event | category | flops | bytes accessed | tf_op | source)
XLA Modules:
  0.0 147.0 jit_solution(10012603302796135666)
XLA Ops:
  0.6 1.3 copy.28
  1.9 0.7 fusion.504
  2.6 0.2 pad.20
  2.8 3.7 %gather_fusion = bf16[4,128,512]{2,0,1:T(4,128)(2,1)} fusion(bf16[4,136,512]{2,0,1:T(4,128)(2,1)S(1)} %pad.20, s32[4]{0:T(128)S(1)} %fusion.504), kind=kCustom, calls=%fused_computation | custom fusion | bytes 1048624 | tf_op jit(solution)/shard_map/vmap()/gather | solution.py:65
  6.5 6.5 %all-to-all-start = ((bf16[8,16,4,512]{3,2,1,0:T(4,128)(2,1)}), bf16[8,16,4,512]{3,2,1,0:T(4,128)(2,1)S(1)}, u32[]{:S(2)}, u32[]{:S(2)}) async-start(bf16[8,16,4,512]{3,2,1,0:T(4,128)(2,1)} %bitcast.3), calls=%async_computation | async-start | bytes 1048576 | tf_op jit(solution)/shard_map/all_to_all | solution.py:97
  13.1 0.0 copy-done.8
  13.1 14.4 %all-to-all-done = bf16[8,16,4,512]{3,2,1,0:T(4,128)(2,1)S(1)} async-done(((bf16[8,16,4,512]{3,2,1,0:T(4,128)(2,1)}), bf16[8,16,4,512]{3,2,1,0:T(4,128)(2,1)S(1)}, u32[]{:S(2)}, u32[]{:S(2)}) %all-to-all-start) | async-done | bytes 524320 | tf_op jit(solution)/shard_map/all_to_all | solution.py:97
  27.5 0.1 fusion.640
  27.7 1.9 %collective-permute-start = (bf16[4,32,512]{2,1,0:T(8,128)(2,1)S(1)}, bf16[4,32,512]{2,1,0:T(8,128)(2,1)S(1)}, u32[]{:S(2)}, u32[]{:S(2)}) collective-permute-start(bf16[4,32,512]{2,1,0:T(8,128)(2,1)S(1)} %slice.190), channel_id=1, source_target_pairs={{0,1},{1,2},{2,3},{3,4},{4,5},{5,6},{6,7},{8,9},{9,10},{10,11},{11... | collective-permute-start | bytes 393224 | tf_op jit(solution)/shard_map/ppermute | solution.py:17
  29.7 0.6 fusion.642
  33.6 0.2 copy.30
  33.8 0.1 squeeze.7
  34.0 2.4 %collective-permute-start.1 = (bf16[4,32,512]{2,1,0:T(8,128)(2,1)S(1)}, bf16[4,32,512]{2,1,0:T(8,128)(2,1)S(1)}, u32[]{:S(2)}, u32[]{:S(2)}) collective-permute-start(bf16[4,32,512]{2,1,0:T(8,128)(2,1)S(1)} %slice.192), channel_id=1, source_target_pairs={{1,0},{2,1},{3,2},{4,3},{5,4},{6,5},{7,6},{9,8},{10,9},{11,10},{12... | collective-permute-start | bytes 393224 | tf_op jit(solution)/shard_map/ppermute | solution.py:20
  36.4 0.0 collective-permute-done
  36.5 3.8 %collective-permute-done.1 = bf16[4,32,512]{2,1,0:T(8,128)(2,1)S(1)} collective-permute-done((bf16[4,32,512]{2,1,0:T(8,128)(2,1)S(1)}, bf16[4,32,512]{2,1,0:T(8,128)(2,1)S(1)}, u32[]{:S(2)}, u32[]{:S(2)}) %collective-permute-start.1) | collective-permute-done | bytes 131104 | tf_op jit(solution)/shard_map/ppermute | solution.py:20
  40.3 2.7 %fusion.50 = f32[24,32,512]{2,1,0:T(8,128)} fusion(bf16[24,32,512]{2,1,0:T(8,128)(2,1)S(1)} %constant_dynamic-update-slice_fusion), kind=kOutput, calls=%fused_computation.92 | convolution fusion | flops 2423259136 | bytes 2359296 | tf_op jit(solution)/shard_map/rsc,co->rso/dot_general | solution.py:82
  43.0 2.7 %fusion.52 = f32[24,32,512]{2,1,0:T(8,128)} fusion(bf16[24,32,512]{2,1,0:T(8,128)(2,1)S(1)} %constant_dynamic-update-slice_fusion), kind=kOutput, calls=%fused_computation.94 | convolution fusion | flops 2423259136 | bytes 2359296 | tf_op jit(solution)/shard_map/rsc,co->rso/dot_general | solution.py:82
  45.7 0.2 constant_dynamic-slice_fusion
  45.9 3.1 %collective-permute-start.2 = (bf16[24,32,6]{2,1,0:T(8,128)(2,1)S(1)}, bf16[24,32,6]{2,1,0:T(8,128)(2,1)S(1)}, u32[]{:S(2)}, u32[]{:S(2)}) collective-permute-start(bf16[24,32,6]{2,1,0:T(8,128)(2,1)S(1)} %get-tuple-element.7), channel_id=1, source_target_pairs={{0,8},{8,16},{16,24},{1,9},{9,17},{17,25},{2,10},{10,18},{18,26},{... | collective-permute-start | bytes 27656 | tf_op jit(solution)/shard_map/ppermute | solution.py:28
  49.0 1.5 %collective-permute-start.3 = (bf16[24,32,6]{2,1,0:T(8,128)(2,1)S(1)}, bf16[24,32,6]{2,1,0:T(8,128)(2,1)S(1)}, u32[]{:S(2)}, u32[]{:S(2)}) collective-permute-start(bf16[24,32,6]{2,1,0:T(8,128)(2,1)S(1)} %get-tuple-element.6), channel_id=1, source_target_pairs={{8,0},{16,8},{24,16},{9,1},{17,9},{25,17},{10,2},{18,10},{26,18},{... | collective-permute-start | bytes 27656 | tf_op jit(solution)/shard_map/ppermute | solution.py:28
  50.5 1.8 %fusion.115 = f32[24,32,260]{2,1,0:T(8,128)S(1)} fusion(bf16[24,32,512]{2,1,0:T(8,128)(2,1)S(1)} %constant_dynamic-update-slice_fusion, s32[260]{0:T(512)S(1)} %pad_add_fusion), kind=kOutput, calls=%fused_computation.140 | convolution fusion | flops 1228963840 | bytes 1586192 | tf_op jit(solution)/shard_map/rsc,co->rso/dot_general | solution.py:82
  52.3 3.8 %copy.37 = f32[24,32,260]{1,0,2:T(8,128)} copy(f32[24,32,260]{2,1,0:T(8,128)S(1)} %fusion.115) | data formatting | bytes 1597440 | tf_op jit(solution)/shard_map/rsc,co->rso/dot_general | solution.py:82
  56.0 1.5 %collective-permute-done.3 = bf16[24,32,6]{2,1,0:T(8,128)(2,1)S(1)} collective-permute-done((bf16[24,32,6]{2,1,0:T(8,128)(2,1)S(1)}, bf16[24,32,6]{2,1,0:T(8,128)(2,1)S(1)}, u32[]{:S(2)}, u32[]{:S(2)}) %collective-permute-start.3) | collective-permute-done | bytes 9248 | tf_op jit(solution)/shard_map/ppermute | solution.py:28
  57.5 0.7 fusion.343
  58.2 3.7 %copy.40 = f32[24,32,260]{1,0,2:T(8,128)} copy(f32[24,32,260]{2,1,0:T(8,128)S(1)} %fusion.343) | data formatting | bytes 1597440 | tf_op jit(solution)/shard_map/rsc,co->rso/dot_general | solution.py:82
  61.9 0.0 collective-permute-done.2
  61.9 0.7 fusion.345
  62.6 0.0 copy-done
  62.6 3.8 %copy.38 = f32[24,32,260]{1,0,2:T(8,128)} copy(f32[24,32,260]{2,1,0:T(8,128)S(1)} %fusion.345) | data formatting | bytes 1597440 | tf_op jit(solution)/shard_map/rsc,co->rso/dot_general | solution.py:82
  66.4 4.2 %add_add_fusion = f32[24,32,260]{1,0,2:T(8,128)S(1)} fusion(f32[24,32,260]{1,0,2:T(8,128)} %copy.40, f32[24,32,260]{1,0,2:T(8,128)} %copy.37, f32[24,32,260]{1,0,2:T(8,128)} %copy.38), kind=kLoop, calls=%fused_computation.1 | loop fusion | flops 399360 | bytes 3194880 | tf_op jit(solution)/shard_map/add | solution.py:83
  70.6 4.1 %slice.231 = f32[8,32,260]{1,0,2:T(8,128)} slice(f32[24,32,260]{1,0,2:T(8,128)S(1)} %add_add_fusion), slice={[6:21:2], [0:32:1], [0:260:1]} | slice | bytes 532480 | tf_op jit(solution)/shard_map/slice | solution.py:50
  74.7 4.1 %slice.230 = f32[8,32,260]{1,0,2:T(8,128)} slice(f32[24,32,260]{1,0,2:T(8,128)S(1)} %add_add_fusion), slice={[5:20:2], [0:32:1], [0:260:1]} | slice | bytes 532480 | tf_op jit(solution)/shard_map/slice | solution.py:50
  78.7 4.0 %slice.229 = f32[8,32,260]{1,0,2:T(8,128)} slice(f32[24,32,260]{1,0,2:T(8,128)S(1)} %add_add_fusion), slice={[4:19:2], [0:32:1], [0:260:1]} | slice | bytes 532480 | tf_op jit(solution)/shard_map/slice | solution.py:50
  82.8 4.0 %slice.228 = f32[8,32,260]{1,0,2:T(8,128)} slice(f32[24,32,260]{1,0,2:T(8,128)S(1)} %add_add_fusion), slice={[3:18:2], [0:32:1], [0:260:1]} | slice | bytes 532480 | tf_op jit(solution)/shard_map/slice | solution.py:50
  86.8 4.1 %slice.227 = f32[8,32,260]{1,0,2:T(8,128)} slice(f32[24,32,260]{1,0,2:T(8,128)S(1)} %add_add_fusion), slice={[2:17:2], [0:32:1], [0:260:1]} | slice | bytes 532480 | tf_op jit(solution)/shard_map/slice | solution.py:45
  90.9 2.8 %multiply_add_fusion.1 = f32[8,32,260]{1,0,2:T(8,128)S(1)} fusion(f32[8,32,260]{1,0,2:T(8,128)} %slice.231, f32[8,32,260]{1,0,2:T(8,128)} %slice.230, f32[8,32,260]{1,0,2:T(8,128)} %slice.229, f32[8,32,260]{1,0,2:T(8,128)} %slice.228, f32[8,32,260]{1,0,2:T(8,128)} %slice.227), kind=kLoop, calls=%fused_computation.22 | loop fusion | flops 599040 | bytes 1597440 | tf_op jit(solution)/shard_map/add | solution.py:53
  93.7 0.3 pad.23
  94.0 6.1 %slice.236 = f32[8,16,260]{1,0,2:T(8,128)S(1)} slice(f32[8,36,260]{1,0,2:T(8,128)S(1)} %pad.23), slice={[0:8:1], [4:35:2], [0:260:1]} | slice | bytes 266240 | tf_op jit(solution)/shard_map/slice | solution.py:50
  100.1 6.1 %slice.235 = f32[8,16,260]{1,0,2:T(8,128)S(1)} slice(f32[8,36,260]{1,0,2:T(8,128)S(1)} %pad.23), slice={[0:8:1], [3:34:2], [0:260:1]} | slice | bytes 266240 | tf_op jit(solution)/shard_map/slice | solution.py:50
  106.2 6.6 %slice.234 = f32[8,16,260]{1,0,2:T(8,128)} slice(f32[8,36,260]{1,0,2:T(8,128)S(1)} %pad.23), slice={[0:8:1], [2:33:2], [0:260:1]} | slice | bytes 266240 | tf_op jit(solution)/shard_map/slice | solution.py:50
  112.7 6.6 %slice.233 = f32[8,16,260]{1,0,2:T(8,128)} slice(f32[8,36,260]{1,0,2:T(8,128)S(1)} %pad.23), slice={[0:8:1], [1:32:2], [0:260:1]} | slice | bytes 266240 | tf_op jit(solution)/shard_map/slice | solution.py:50
  119.3 6.4 %slice.232 = f32[8,16,260]{1,0,2:T(8,128)} slice(f32[8,36,260]{1,0,2:T(8,128)S(1)} %pad.23), slice={[0:8:1], [0:31:2], [0:260:1]} | slice | bytes 266240 | tf_op jit(solution)/shard_map/slice | solution.py:45
  125.7 2.2 %multiply_add_fusion = bf16[8,16,260]{1,0,2:T(8,128)(2,1)S(1)} fusion(f32[8,16,260]{1,0,2:T(8,128)S(1)} %slice.236, f32[8,16,260]{1,0,2:T(8,128)S(1)} %slice.235, f32[8,16,260]{1,0,2:T(8,128)} %slice.234, f32[8,16,260]{1,0,2:T(8,128)} %slice.233, f32[8,16,260]{1,0,2:T(8,128)} %slice.232), kind=kLoop, calls=%fused_computation.21 | loop fusion | flops 332800 | bytes 732160 | tf_op jit(solution)/shard_map/add | solution.py:53
  127.9 0.0 copy-start.6
  127.9 0.0 copy-start.1
  128.0 0.3 copy.43
  128.3 0.1 fusion.208
  128.4 0.4 fusion.176
  128.7 0.2 convolution_add_fusion
  129.0 1.9 %collective-permute-start.5 = (f32[2,16,128]{2,1,0:T(8,128)S(1)}, f32[2,16,128]{2,1,0:T(8,128)S(1)}, u32[]{:S(2)}, u32[]{:S(2)}) collective-permute-start(f32[2,16,128]{2,1,0:T(8,128)S(1)} %get-tuple-element.11), channel_id=1, source_target_pairs={{1,0},{2,1},{3,2},{4,3},{5,4},{6,5},{7,6},{9,8},{10,9},{11,10},{12... | collective-permute-start | bytes 49160 | tf_op jit(solution)/shard_map/ppermute | solution.py:20
  130.9 5.2 %collective-permute-start.4 = (f32[2,16,128]{2,1,0:T(8,128)S(1)}, f32[2,16,128]{2,1,0:T(8,128)S(1)}, u32[]{:S(2)}, u32[]{:S(2)}) collective-permute-start(f32[2,16,128]{2,1,0:T(8,128)S(1)} %get-tuple-element.10), channel_id=1, source_target_pairs={{0,1},{1,2},{2,3},{3,4},{4,5},{5,6},{6,7},{8,9},{9,10},{10,11},{11... | collective-permute-start | bytes 49160 | tf_op jit(solution)/shard_map/ppermute | solution.py:17
  136.1 0.8 fusion.213
  137.0 0.0 copy-done.4
  137.0 0.0 copy-start.3
  137.0 0.8 fusion.219
  137.8 0.6 copy-done.3
  138.4 1.0 add_add_fusion.1
  139.4 0.4 copy-done.2
  139.8 0.9 add_add_fusion.2
  140.7 2.5 %fusion.34 = (f32[16,32,512]{2,1,0:T(8,128)S(1)}, f32[16,32,512]{2,1,0:T(8,128)S(1)}) fusion(f32[24,32,512]{2,1,0:T(8,128)S(1)} %add_add_fusion.1, f32[24,32,512]{2,1,0:T(8,128)S(1)} %add_add_fusion.2), kind=kLoop, calls=%fused_computation.59 | loop fusion | flops 8912896 | bytes 20971520 | tf_op jit(solution)/shard_map/add | solution.py:53
  143.3 3.0 %fusion.10 = bf16[16,32,512]{2,1,0:T(8,128)(2,1)} fusion(f32[16,32,512]{2,1,0:T(8,128)S(1)} %get-tuple-element.15, f32[16,32,512]{2,1,0:T(8,128)S(1)} %get-tuple-element.14), kind=kLoop, calls=%fused_computation.33 | loop fusion | flops 9437184 | bytes 2621440 | tf_op jit(solution)/shard_map/convert_element_type | solution.py:122
  146.3 0.0 collective-permute-done.5
  146.3 0.0 collective-permute-done.4
  146.4 0.6 add_convert_fusion
  (36 shorter events, 0.4 us)
Async XLA Ops:
  6.5 6.6 %copy-start.8 = (pred[4]{0:T(512)(128)(4,1)S(1)}, pred[4]{0:T(512)(128)(4,1)}, u32[]{:S(2)}) copy-start(pred[4]{0:T(512)(128)(4,1)} %constant.255) | copy-start | bytes 16
  6.5 6.6 %copy-start.9 = (pred[4]{0:T(512)(128)(4,1)S(1)}, pred[4]{0:T(512)(128)(4,1)}, u32[]{:S(2)}) copy-start(pred[4]{0:T(512)(128)(4,1)} %constant.254) | copy-start | bytes 16
  6.5 23.2 %copy-start.5 = (s32[3]{0:T(128)S(1)}, s32[3]{0:T(128)}, u32[]{:S(2)}) copy-start(s32[3]{0:T(128)} %param.7) | copy-start | bytes 40
  6.5 27.0 %copy-start.7 = (s32[4]{0:T(128)S(1)}, s32[4]{0:T(128)}, u32[]{:S(2)}) copy-start(s32[4]{0:T(128)} %constant.238.clone) | copy-start | bytes 52
  6.5 21.0 %all-to-all-start = ((bf16[8,16,4,512]{3,2,1,0:T(4,128)(2,1)}), bf16[8,16,4,512]{3,2,1,0:T(4,128)(2,1)S(1)}, u32[]{:S(2)}, u32[]{:S(2)}) async-start(bf16[8,16,4,512]{3,2,1,0:T(4,128)(2,1)} %bitcast.3), calls=%async_computation | async-start | bytes 1048576 | tf_op jit(solution)/shard_map/all_to_all | solution.py:97
  27.7 8.7 %collective-permute-start = (bf16[4,32,512]{2,1,0:T(8,128)(2,1)S(1)}, bf16[4,32,512]{2,1,0:T(8,128)(2,1)S(1)}, u32[]{:S(2)}, u32[]{:S(2)}) collective-permute-start(bf16[4,32,512]{2,1,0:T(8,128)(2,1)S(1)} %slice.190), channel_id=1, source_target_pairs={{0,1},{1,2},{2,3},{3,4},{4,5},{5,6},{6,7},{8,9},{9,10},{10,11},{11... | collective-permute-start | bytes 393224 | tf_op jit(solution)/shard_map/ppermute | solution.py:17
  34.0 6.3 %collective-permute-start.1 = (bf16[4,32,512]{2,1,0:T(8,128)(2,1)S(1)}, bf16[4,32,512]{2,1,0:T(8,128)(2,1)S(1)}, u32[]{:S(2)}, u32[]{:S(2)}) collective-permute-start(bf16[4,32,512]{2,1,0:T(8,128)(2,1)S(1)} %slice.192), channel_id=1, source_target_pairs={{1,0},{2,1},{3,2},{4,3},{5,4},{6,5},{7,6},{9,8},{10,9},{11,10},{12... | collective-permute-start | bytes 393224 | tf_op jit(solution)/shard_map/ppermute | solution.py:20
  45.9 16.0 %collective-permute-start.2 = (bf16[24,32,6]{2,1,0:T(8,128)(2,1)S(1)}, bf16[24,32,6]{2,1,0:T(8,128)(2,1)S(1)}, u32[]{:S(2)}, u32[]{:S(2)}) collective-permute-start(bf16[24,32,6]{2,1,0:T(8,128)(2,1)S(1)} %get-tuple-element.7), channel_id=1, source_target_pairs={{0,8},{8,16},{16,24},{1,9},{9,17},{17,25},{2,10},{10,18},{18,26},{... | collective-permute-start | bytes 27656 | tf_op jit(solution)/shard_map/ppermute | solution.py:28
  49.0 8.5 %collective-permute-start.3 = (bf16[24,32,6]{2,1,0:T(8,128)(2,1)S(1)}, bf16[24,32,6]{2,1,0:T(8,128)(2,1)S(1)}, u32[]{:S(2)}, u32[]{:S(2)}) collective-permute-start(bf16[24,32,6]{2,1,0:T(8,128)(2,1)S(1)} %get-tuple-element.6), channel_id=1, source_target_pairs={{8,0},{16,8},{24,16},{9,1},{17,9},{25,17},{10,2},{18,10},{26,18},{... | collective-permute-start | bytes 27656 | tf_op jit(solution)/shard_map/ppermute | solution.py:28
  61.9 0.7 copy-start
  127.9 0.8 copy-start.6
  127.9 8.2 %copy-start.1 = (bf16[24,32,6]{2,1,0:T(8,128)(2,1)S(1)}, bf16[24,32,6]{2,1,0:T(8,128)(2,1)}, u32[]{:S(2)}) copy-start(bf16[24,32,6]{2,1,0:T(8,128)(2,1)} %copy-done) | copy-start | bytes 27652
  128.3 8.7 %copy-start.4 = (bf16[8,16,256]{2,1,0:T(8,128)(2,1)}, bf16[8,16,256]{2,1,0:T(8,128)(2,1)S(1)}, u32[]{:S(2)}) copy-start(bf16[8,16,256]{2,1,0:T(8,128)(2,1)S(1)} %copy.43) | copy-start | bytes 196612
  129.0 17.3 %collective-permute-start.5 = (f32[2,16,128]{2,1,0:T(8,128)S(1)}, f32[2,16,128]{2,1,0:T(8,128)S(1)}, u32[]{:S(2)}, u32[]{:S(2)}) collective-permute-start(f32[2,16,128]{2,1,0:T(8,128)S(1)} %get-tuple-element.11), channel_id=1, source_target_pairs={{1,0},{2,1},{3,2},{4,3},{5,4},{6,5},{7,6},{9,8},{10,9},{11,10},{12... | collective-permute-start | bytes 49160 | tf_op jit(solution)/shard_map/ppermute | solution.py:20
  130.9 15.4 %collective-permute-start.4 = (f32[2,16,128]{2,1,0:T(8,128)S(1)}, f32[2,16,128]{2,1,0:T(8,128)S(1)}, u32[]{:S(2)}, u32[]{:S(2)}) collective-permute-start(f32[2,16,128]{2,1,0:T(8,128)S(1)} %get-tuple-element.10), channel_id=1, source_target_pairs={{0,1},{1,2},{2,3},{3,4},{4,5},{5,6},{6,7},{8,9},{9,10},{10,11},{11... | collective-permute-start | bytes 49160 | tf_op jit(solution)/shard_map/ppermute | solution.py:17
  137.0 1.4 copy-start.3
  138.4 1.4 copy-start.2
where the time goes:
time: 148 us; the launch traced here: 147 us
  local copies, waits for them, and re-layouts  71.6 us (48%)
  starting transfers between devices  22.6 us (15%)
  waiting for transfers between devices  19.7 us (13%)
  other arithmetic  16.2 us (11%)
  matrix products  12.6 us (9%)
  between operations  4.31 us (3%)
    slice x12, local copies, waits for them, and re-layouts, smooth(): lax.slice_in_dim(source, lowest, lowest + (length_out - 1) * stride + 1,...  41.5 us
    all_to_all x1, waiting for transfers between devices, body(): lax.all_to_all(outgoing, 'slab', split_axis=0, concat_axis=2, tiled=True)[0]  14.4 us
    dot_general x11, matrix products, along_columns(): jnp.einsum('rsc,co->rso', piece_field, table, precision=lax.Precision.HIG...  12.6 us
    dot_general x3, local copies, waits for them, and re-layouts, along_columns(): jnp.einsum('rsc,co->rso', piece_field, table, precision=lax.Precision.HIG...  11.3 us
    slice x3, local copies, waits for them, and re-layouts, smooth(): lax.slice_in_dim(source, begin_at, begin_at + (length_out - 1) * stride +...  10.4 us
    add x4, other arithmetic, smooth(): result = result + weights[offset] * window  7.57 us
    ppermute x2, starting transfers between devices, padded_2(): lax.ppermute(lax.slice_in_dim(block, block.shape[dim] - width, None, axis...  7.1 us
    all_to_all x1, starting transfers between devices, body(): lax.all_to_all(outgoing, 'slab', split_axis=0, concat_axis=2, tiled=True)[0]  6.52 us
  transfers between devices with their start and end apart: 7, of which 3 were waited for; matrix products, arithmetic and copies ran while one was open for 14% of the time, Pallas kernels for 0%

commit v1 on v0

--- a/solution.py
+++ b/solution.py
@@ -3,6 +3,7 @@
 import jax.numpy as jnp
 from jax import lax
 from jax.sharding import PartitionSpec as P
+from jax.lax import axis_index, ppermute, psum
 
 SLAB_ROWS = 16
 STRIP = 6
@@ -94,7 +95,26 @@
     row_depth = RADIUS
     deskewed = deskew(raw_stack, shear_offsets, shear_top, total_rows, 0)
     outgoing = deskewed.reshape(slab_count, SLAB_ROWS, planes, columns)
-    volume = lax.all_to_all(outgoing, "slab", split_axis=0, concat_axis=2, tiled=True)[0]
+
+    def _start_map(tile_in, comm_axis):
+        all_values, tall = (psum(1, comm_axis), axis_index(comm_axis))
+        heard = tile_in.shape[0] // all_values
+        state_next = list(tile_in.shape)
+        state_next[0] = heard
+        x_now = state_next[2]
+        state_next[2] = x_now * all_values
+        z = jnp.zeros(state_next, tile_in.dtype)
+        for src_i in range(all_values):
+            y = lax.dynamic_slice_in_dim(tile_in, (tall ^ src_i) * heard, heard, axis=0)
+            if src_i:
+                cards = []
+                for h in range(all_values):
+                    cards.append((h, h ^ src_i))
+                y = ppermute(y, comm_axis, cards)
+            z = lax.dynamic_update_slice_in_dim(z, y, (tall ^ src_i) * x_now, axis=2)
+        return z
+
+    volume = _start_map(outgoing, "slab")[0]
     volume = padded_2(volume, (("slab", 0),), row_depth)
     right_width = intersection_widths[jnp.minimum(tile_index, tile_count - 2)]
     left_width = intersection_widths[jnp.maximum(tile_index - 1, 0)]

time: 148 us -> 139 us (0.939)
  waiting for transfers between devices: 19.7 us -> 6.02 us
  starting transfers between devices: 22.6 us -> 26.7 us
    all_to_all x1 -> x0, waiting for transfers between devices: 14.4 us -> none  [body(): lax.all_to_all(outgoing, 'slab', split_axis=0, concat_axis=2, tiled=True)[0]]
    ppermute x0 -> x7, starting transfers between devices: none -> 9.67 us  [_start_map(): y = ppermute(y, comm_axis, cards)]
    all_to_all x1 -> x0, starting transfers between devices: 6.52 us -> none  [body(): lax.all_to_all(outgoing, 'slab', split_axis=0, concat_axis=2, tiled=True)[0]]
    ppermute x0 -> x7, waiting for transfers between devices: none -> 6 us  [_start_map(): y = ppermute(y, comm_axis, cards)]
    ppermute x2, waiting for transfers between devices: 3.79 us -> 0.01 us  [padded_2(): lax.ppermute(lax.slice_in_dim(block, 0, width, axis=dim), axis, backward)]
  transfers between devices with their start and end apart: 7 -> 13, of which waited for: 3 -> 1; matrix products, arithmetic and copies ran while one was open for 14% -> 19% of each run, Pallas kernels for 0% -> 0%
where the time goes in v1:
time: 139 us; the launch traced here: 137 us
  local copies, waits for them, and re-layouts  71 us (51%)
  starting transfers between devices  26.7 us (19%)
  other arithmetic  16.5 us (12%)
  matrix products  12.7 us (9%)
  waiting for transfers between devices  6.02 us (4%)
  between operations  4.48 us (3%)
    slice x12, local copies, waits for them, and re-layouts, smooth(): lax.slice_in_dim(source, lowest, lowest + (length_out - 1) * stride + 1,...  41.5 us
    dot_general x11, matrix products, along_columns(): jnp.einsum('rsc,co->rso', piece_field, table, precision=lax.Precision.HIG...  12.7 us
    dot_general x3, local copies, waits for them, and re-layouts, along_columns(): jnp.einsum('rsc,co->rso', piece_field, table, precision=lax.Precision.HIG...  11.4 us
    slice x3, local copies, waits for them, and re-layouts, smooth(): lax.slice_in_dim(source, begin_at, begin_at + (length_out - 1) * stride +...  10.5 us
    ppermute x7, starting transfers between devices, _start_map(): y = ppermute(y, comm_axis, cards)  9.67 us
    ppermute x2, starting transfers between devices, padded_2(): lax.ppermute(lax.slice_in_dim(block, block.shape[dim] - width, None, axis...  8.4 us
    add x4, other arithmetic, smooth(): result = result + weights[offset] * window  7.79 us
    ppermute x7, waiting for transfers between devices, _start_map(): y = ppermute(y, comm_axis, cards)  6 us
  transfers between devices with their start and end apart: 13, of which 1 were waited for; matrix products, arithmetic and copies ran while one was open for 19% of the time, Pallas kernels for 0%

profile of v1, /device:TPU:1, one launch (start us, length us, event | category | flops | bytes accessed | tf_op | source)
XLA Modules:
  0.0 137.4 jit_solution(4577545920242930509)
XLA Ops:
  0.7 1.3 copy.16
  1.9 0.7 fusion.514
  2.6 0.2 pad.20
  2.8 3.0 %gather_fusion = bf16[4,128,512]{2,0,1:T(4,128)(2,1)S(1)} fusion(bf16[4,136,512]{2,0,1:T(4,128)(2,1)S(1)} %pad.20, s32[4]{0:T(128)S(1)} %fusion.514), kind=kCustom, calls=%fused_computation | custom fusion | bytes 1048624 | tf_op jit(solution)/shard_map/vmap()/gather | solution.py:66
  5.8 0.0 copy-start.8
  5.8 0.0 copy-start.9
  5.8 0.2 constant_dynamic-slice_fusion.2
  6.0 0.1 collective-permute-start
  6.2 2.8 %collective-permute-start.1 = (bf16[1,16,4,512]{3,2,1,0:T(4,128)(2,1)S(1)}, bf16[1,16,4,512]{3,2,1,0:T(4,128)(2,1)S(1)}, u32[]{:S(2)}, u32[]{:S(2)}) collective-permute-start(bf16[1,16,4,512]{3,2,1,0:T(4,128)(2,1)S(1)} %get-tuple-element.15), channel_id=1, source_target_pairs={{0,2},{1,3},{2,0},{3,1},{4,6},{5,7},{6,4},{7,5},{8,10},{9,11},{10,... | collective-permute-start | bytes 196616 | tf_op jit(solution)/shard_map/ppermute | solution.py:113
  8.9 0.0 collective-permute-start.2
  9.0 2.7 %collective-permute-start.3 = (bf16[1,16,4,512]{3,2,1,0:T(4,128)(2,1)S(1)}, bf16[1,16,4,512]{3,2,1,0:T(4,128)(2,1)S(1)}, u32[]{:S(2)}, u32[]{:S(2)}) collective-permute-start(bf16[1,16,4,512]{3,2,1,0:T(4,128)(2,1)S(1)} %get-tuple-element.13), channel_id=1, source_target_pairs={{0,4},{1,5},{2,6},{3,7},{4,0},{5,1},{6,2},{7,3},{8,12},{9,13},{10,... | collective-permute-start | bytes 196616 | tf_op jit(solution)/shard_map/ppermute | solution.py:113
  11.6 0.2 collective-permute-start.4
  11.9 0.1 bitcast_dynamic-update-slice_fusion.7
  12.1 3.5 %collective-permute-start.5 = (bf16[1,16,4,512]{3,2,1,0:T(4,128)(2,1)S(1)}, bf16[1,16,4,512]{3,2,1,0:T(4,128)(2,1)S(1)}, u32[]{:S(2)}, u32[]{:S(2)}) collective-permute-start(bf16[1,16,4,512]{3,2,1,0:T(4,128)(2,1)S(1)} %get-tuple-element.11), channel_id=1, source_target_pairs={{0,6},{1,7},{2,4},{3,5},{4,2},{5,3},{6,0},{7,1},{8,14},{9,15},{10,... | collective-permute-start | bytes 196616 | tf_op jit(solution)/shard_map/ppermute | solution.py:113
  15.7 0.3 collective-permute-start.6
  16.0 0.1 bitcast_dynamic-update-slice_fusion.4
  16.1 0.1 bitcast_dynamic-update-slice_fusion.3
  16.2 6.0 %collective-permute-done.4 = bf16[1,16,4,512]{3,2,1,0:T(4,128)(2,1)S(1)} collective-permute-done((bf16[1,16,4,512]{3,2,1,0:T(4,128)(2,1)S(1)}, bf16[1,16,4,512]{3,2,1,0:T(4,128)(2,1)S(1)}, u32[]{:S(2)}, u32[]{:S(2)}) %collective-permute-start.4) | collective-permute-done | bytes 65568 | tf_op jit(solution)/shard_map/ppermute | solution.py:113
  22.2 0.1 bitcast_dynamic-update-slice_fusion.1
  22.3 0.1 bitcast_dynamic-update-slice_fusion
  22.4 2.3 %collective-permute-start.8 = (bf16[4,32,512]{2,1,0:T(8,128)(2,1)S(1)}, bf16[4,32,512]{2,1,0:T(8,128)(2,1)S(1)}, u32[]{:S(2)}, u32[]{:S(2)}) collective-permute-start(bf16[4,32,512]{2,1,0:T(8,128)(2,1)S(1)} %get-tuple-element.9), channel_id=1, source_target_pairs={{1,0},{2,1},{3,2},{4,3},{5,4},{6,5},{7,6},{9,8},{10,9},{11,10},{12... | collective-permute-start | bytes 393224 | tf_op jit(solution)/shard_map/ppermute | solution.py:21
  24.7 4.8 %collective-permute-start.7 = (bf16[4,32,512]{2,1,0:T(8,128)(2,1)S(1)}, bf16[4,32,512]{2,1,0:T(8,128)(2,1)S(1)}, u32[]{:S(2)}, u32[]{:S(2)}) collective-permute-start(bf16[4,32,512]{2,1,0:T(8,128)(2,1)S(1)} %get-tuple-element.8), channel_id=1, source_target_pairs={{0,1},{1,2},{2,3},{3,4},{4,5},{5,6},{6,7},{8,9},{9,10},{10,11},{11... | collective-permute-start | bytes 393224 | tf_op jit(solution)/shard_map/ppermute | solution.py:18
  29.5 0.6 fusion.641
  33.4 0.1 pad_maximum_fusion
  33.5 0.2 constant_dynamic-slice_fusion
  33.7 3.1 %collective-permute-start.9 = (bf16[24,32,6]{2,1,0:T(8,128)(2,1)S(1)}, bf16[24,32,6]{2,1,0:T(8,128)(2,1)S(1)}, u32[]{:S(2)}, u32[]{:S(2)}) collective-permute-start(bf16[24,32,6]{2,1,0:T(8,128)(2,1)S(1)} %get-tuple-element.7), channel_id=1, source_target_pairs={{0,8},{8,16},{16,24},{1,9},{9,17},{17,25},{2,10},{10,18},{18,26},{... | collective-permute-start | bytes 27656 | tf_op jit(solution)/shard_map/ppermute | solution.py:29
  36.8 1.3 collective-permute-start.10
  38.1 2.7 %fusion.50 = f32[24,32,512]{2,1,0:T(8,128)} fusion(bf16[4,32,512]{2,1,0:T(8,128)(2,1)S(1)} %collective-permute-done.8, bf16[16,32,512]{2,1,0:T(8,128)(2,1)S(1)} %bitcast_dynamic-update-slice_fusion, bf16[4,32,512]{2,1,0:T(8,128)(2,1)S(1)} %collective-permute-done.7), kind=kOutput, calls=%fused_computation.92 | convolution fusion | flops 2424045568 | bytes 2359296 | tf_op jit(solution)/shard_map/rsc,co->rso/dot_general | solution.py:83
  40.8 2.7 %fusion.52 = f32[24,32,512]{2,1,0:T(8,128)} fusion(bf16[4,32,512]{2,1,0:T(8,128)(2,1)S(1)} %collective-permute-done.8, bf16[16,32,512]{2,1,0:T(8,128)(2,1)S(1)} %bitcast_dynamic-update-slice_fusion, bf16[4,32,512]{2,1,0:T(8,128)(2,1)S(1)} %collective-permute-done.7), kind=kOutput, calls=%fused_computation.94 | convolution fusion | flops 2424045568 | bytes 2359296 | tf_op jit(solution)/shard_map/rsc,co->rso/dot_general | solution.py:83
  43.5 1.8 %fusion.115 = f32[24,32,260]{2,1,0:T(8,128)S(1)} fusion(s32[260]{0:T(512)S(1)} %pad_add_fusion, bf16[4,32,512]{2,1,0:T(8,128)(2,1)S(1)} %collective-permute-done.8, bf16[16,32,512]{2,1,0:T(8,128)(2,1)S(1)} %bitcast_dynamic-update-slice_fusion, bf16[4,32,512]{2,1,0:T(8,128)(2,1)S(1)} %collective-permute-done.7), kind=kOutput, calls=%fused_computation.141 | convolution fusion | flops 1229750272 | bytes 1586192 | tf_op jit(solution)/shard_map/rsc,co->rso/dot_general | solution.py:83
  45.3 3.9 %copy.22 = f32[24,32,260]{1,0,2:T(8,128)} copy(f32[24,32,260]{2,1,0:T(8,128)S(1)} %fusion.115) | data formatting | bytes 1597440 | tf_op jit(solution)/shard_map/rsc,co->rso/dot_general | solution.py:83
  49.2 0.7 fusion.343
  49.9 3.7 %copy.25 = f32[24,32,260]{1,0,2:T(8,128)} copy(f32[24,32,260]{2,1,0:T(8,128)S(1)} %fusion.343) | data formatting | bytes 1597440 | tf_op jit(solution)/shard_map/rsc,co->rso/dot_general | solution.py:83
  53.6 0.7 fusion.345
  54.3 3.8 %copy.23 = f32[24,32,260]{1,0,2:T(8,128)} copy(f32[24,32,260]{2,1,0:T(8,128)S(1)} %fusion.345) | data formatting | bytes 1597440 | tf_op jit(solution)/shard_map/rsc,co->rso/dot_general | solution.py:83
  58.1 4.2 %add_add_fusion = f32[24,32,260]{1,0,2:T(8,128)S(1)} fusion(f32[24,32,260]{1,0,2:T(8,128)} %copy.25, f32[24,32,260]{1,0,2:T(8,128)} %copy.22, f32[24,32,260]{1,0,2:T(8,128)} %copy.23), kind=kLoop, calls=%fused_computation.1 | loop fusion | flops 399360 | bytes 3194880 | tf_op jit(solution)/shard_map/add | solution.py:84
  62.3 4.1 %slice.223 = f32[8,32,260]{1,0,2:T(8,128)} slice(f32[24,32,260]{1,0,2:T(8,128)S(1)} %add_add_fusion), slice={[6:21:2], [0:32:1], [0:260:1]} | slice | bytes 532480 | tf_op jit(solution)/shard_map/slice | solution.py:51
  66.4 4.0 %slice.222 = f32[8,32,260]{1,0,2:T(8,128)} slice(f32[24,32,260]{1,0,2:T(8,128)S(1)} %add_add_fusion), slice={[5:20:2], [0:32:1], [0:260:1]} | slice | bytes 532480 | tf_op jit(solution)/shard_map/slice | solution.py:51
  70.4 4.0 %slice.221 = f32[8,32,260]{1,0,2:T(8,128)} slice(f32[24,32,260]{1,0,2:T(8,128)S(1)} %add_add_fusion), slice={[4:19:2], [0:32:1], [0:260:1]} | slice | bytes 532480 | tf_op jit(solution)/shard_map/slice | solution.py:51
  74.5 4.0 %slice.220 = f32[8,32,260]{1,0,2:T(8,128)} slice(f32[24,32,260]{1,0,2:T(8,128)S(1)} %add_add_fusion), slice={[3:18:2], [0:32:1], [0:260:1]} | slice | bytes 532480 | tf_op jit(solution)/shard_map/slice | solution.py:51
  78.5 4.1 %slice.219 = f32[8,32,260]{1,0,2:T(8,128)} slice(f32[24,32,260]{1,0,2:T(8,128)S(1)} %add_add_fusion), slice={[2:17:2], [0:32:1], [0:260:1]} | slice | bytes 532480 | tf_op jit(solution)/shard_map/slice | solution.py:46
  82.6 2.8 %multiply_add_fusion.1 = f32[8,32,260]{1,0,2:T(8,128)S(1)} fusion(f32[8,32,260]{1,0,2:T(8,128)} %slice.223, f32[8,32,260]{1,0,2:T(8,128)} %slice.222, f32[8,32,260]{1,0,2:T(8,128)} %slice.221, f32[8,32,260]{1,0,2:T(8,128)} %slice.220, f32[8,32,260]{1,0,2:T(8,128)} %slice.219), kind=kLoop, calls=%fused_computation.22 | loop fusion | flops 599040 | bytes 1597440 | tf_op jit(solution)/shard_map/add | solution.py:54
  85.4 0.3 pad.23
  85.8 6.1 %slice.228 = f32[8,16,260]{1,0,2:T(8,128)S(1)} slice(f32[8,36,260]{1,0,2:T(8,128)S(1)} %pad.23), slice={[0:8:1], [4:35:2], [0:260:1]} | slice | bytes 266240 | tf_op jit(solution)/shard_map/slice | solution.py:51
  91.8 6.1 %slice.227 = f32[8,16,260]{1,0,2:T(8,128)S(1)} slice(f32[8,36,260]{1,0,2:T(8,128)S(1)} %pad.23), slice={[0:8:1], [3:34:2], [0:260:1]} | slice | bytes 266240 | tf_op jit(solution)/shard_map/slice | solution.py:51
  97.9 6.6 %slice.226 = f32[8,16,260]{1,0,2:T(8,128)} slice(f32[8,36,260]{1,0,2:T(8,128)S(1)} %pad.23), slice={[0:8:1], [2:33:2], [0:260:1]} | slice | bytes 266240 | tf_op jit(solution)/shard_map/slice | solution.py:51
  104.5 6.5 %slice.225 = f32[8,16,260]{1,0,2:T(8,128)} slice(f32[8,36,260]{1,0,2:T(8,128)S(1)} %pad.23), slice={[0:8:1], [1:32:2], [0:260:1]} | slice | bytes 266240 | tf_op jit(solution)/shard_map/slice | solution.py:51
  111.0 6.4 %slice.224 = f32[8,16,260]{1,0,2:T(8,128)} slice(f32[8,36,260]{1,0,2:T(8,128)S(1)} %pad.23), slice={[0:8:1], [0:31:2], [0:260:1]} | slice | bytes 266240 | tf_op jit(solution)/shard_map/slice | solution.py:46
  117.4 2.2 %multiply_add_fusion = bf16[8,16,260]{1,0,2:T(8,128)(2,1)S(1)} fusion(f32[8,16,260]{1,0,2:T(8,128)S(1)} %slice.228, f32[8,16,260]{1,0,2:T(8,128)S(1)} %slice.227, f32[8,16,260]{1,0,2:T(8,128)} %slice.226, f32[8,16,260]{1,0,2:T(8,128)} %slice.225, f32[8,16,260]{1,0,2:T(8,128)} %slice.224), kind=kLoop, calls=%fused_computation.21 | loop fusion | flops 332800 | bytes 732160 | tf_op jit(solution)/shard_map/add | solution.py:54
  119.7 0.3 copy.28
  120.0 0.1 fusion.208
  120.1 0.4 fusion.176
  120.5 0.2 convolution_add_fusion
  120.7 1.9 %collective-permute-start.12 = (f32[2,16,128]{2,1,0:T(8,128)S(1)}, f32[2,16,128]{2,1,0:T(8,128)S(1)}, u32[]{:S(2)}, u32[]{:S(2)}) collective-permute-start(f32[2,16,128]{2,1,0:T(8,128)S(1)} %get-tuple-element.18), channel_id=1, source_target_pairs={{1,0},{2,1},{3,2},{4,3},{5,4},{6,5},{7,6},{9,8},{10,9},{11,10},{12... | collective-permute-start | bytes 49160 | tf_op jit(solution)/shard_map/ppermute | solution.py:21
  122.7 3.6 %collective-permute-start.11 = (f32[2,16,128]{2,1,0:T(8,128)S(1)}, f32[2,16,128]{2,1,0:T(8,128)S(1)}, u32[]{:S(2)}, u32[]{:S(2)}) collective-permute-start(f32[2,16,128]{2,1,0:T(8,128)S(1)} %get-tuple-element.17), channel_id=1, source_target_pairs={{0,1},{1,2},{2,3},{3,4},{4,5},{5,6},{6,7},{8,9},{9,10},{10,11},{11... | collective-permute-start | bytes 49160 | tf_op jit(solution)/shard_map/ppermute | solution.py:18
  126.3 0.8 fusion.213
  127.2 0.8 fusion.219
  128.0 0.5 copy-done.3
  128.6 1.0 add_add_fusion.1
  129.6 0.4 copy-done.2
  130.0 0.9 add_add_fusion.2
  130.9 2.7 %fusion.34 = (f32[16,32,512]{2,1,0:T(8,128)S(1)}, f32[16,32,512]{2,1,0:T(8,128)S(1)}) fusion(f32[24,32,512]{2,1,0:T(8,128)S(1)} %add_add_fusion.1, f32[24,32,512]{2,1,0:T(8,128)S(1)} %add_add_fusion.2), kind=kLoop, calls=%fused_computation.59 | loop fusion | flops 8912896 | bytes 20971520 | tf_op jit(solution)/shard_map/add | solution.py:54
  133.7 3.0 %fusion.10 = bf16[16,32,512]{2,1,0:T(8,128)(2,1)} fusion(f32[16,32,512]{2,1,0:T(8,128)S(1)} %get-tuple-element.22, f32[16,32,512]{2,1,0:T(8,128)S(1)} %get-tuple-element.21), kind=kLoop, calls=%fused_computation.33 | loop fusion | flops 9437184 | bytes 2621440 | tf_op jit(solution)/shard_map/convert_element_type | solution.py:142
  136.8 0.6 add_convert_fusion
  (50 shorter events, 0.4 us)
Async XLA Ops:
  5.8 6.2 %copy-start.8 = (pred[4]{0:T(512)(128)(4,1)S(1)}, pred[4]{0:T(512)(128)(4,1)}, u32[]{:S(2)}) copy-start(pred[4]{0:T(512)(128)(4,1)} %constant.273) | copy-start | bytes 16
  5.8 6.2 %copy-start.9 = (pred[4]{0:T(512)(128)(4,1)S(1)}, pred[4]{0:T(512)(128)(4,1)}, u32[]{:S(2)}) copy-start(pred[4]{0:T(512)(128)(4,1)} %constant.272) | copy-start | bytes 16
  6.0 6.0 %collective-permute-start = (bf16[1,16,4,512]{3,2,1,0:T(4,128)(2,1)S(1)}, bf16[1,16,4,512]{3,2,1,0:T(4,128)(2,1)S(1)}, u32[]{:S(2)}, u32[]{:S(2)}) collective-permute-start(bf16[1,16,4,512]{3,2,1,0:T(4,128)(2,1)S(1)} %get-tuple-element.16), channel_id=1, source_target_pairs={{0,1},{1,0},{2,3},{3,2},{4,5},{5,4},{6,7},{7,6},{8,9},{9,8},{10,11... | collective-permute-start | bytes 196616 | tf_op jit(solution)/shard_map/ppermute | solution.py:113
  6.2 9.5 %collective-permute-start.1 = (bf16[1,16,4,512]{3,2,1,0:T(4,128)(2,1)S(1)}, bf16[1,16,4,512]{3,2,1,0:T(4,128)(2,1)S(1)}, u32[]{:S(2)}, u32[]{:S(2)}) collective-permute-start(bf16[1,16,4,512]{3,2,1,0:T(4,128)(2,1)S(1)} %get-tuple-element.15), channel_id=1, source_target_pairs={{0,2},{1,3},{2,0},{3,1},{4,6},{5,7},{6,4},{7,5},{8,10},{9,11},{10,... | collective-permute-start | bytes 196616 | tf_op jit(solution)/shard_map/ppermute | solution.py:113
  8.9 7.1 %collective-permute-start.2 = (bf16[1,16,4,512]{3,2,1,0:T(4,128)(2,1)S(1)}, bf16[1,16,4,512]{3,2,1,0:T(4,128)(2,1)S(1)}, u32[]{:S(2)}, u32[]{:S(2)}) collective-permute-start(bf16[1,16,4,512]{3,2,1,0:T(4,128)(2,1)S(1)} %get-tuple-element.14), channel_id=1, source_target_pairs={{0,3},{1,2},{2,1},{3,0},{4,7},{5,6},{6,5},{7,4},{8,11},{9,10},{10,... | collective-permute-start | bytes 196616 | tf_op jit(solution)/shard_map/ppermute | solution.py:113
  9.0 7.1 %collective-permute-start.3 = (bf16[1,16,4,512]{3,2,1,0:T(4,128)(2,1)S(1)}, bf16[1,16,4,512]{3,2,1,0:T(4,128)(2,1)S(1)}, u32[]{:S(2)}, u32[]{:S(2)}) collective-permute-start(bf16[1,16,4,512]{3,2,1,0:T(4,128)(2,1)S(1)} %get-tuple-element.13), channel_id=1, source_target_pairs={{0,4},{1,5},{2,6},{3,7},{4,0},{5,1},{6,2},{7,3},{8,12},{9,13},{10,... | collective-permute-start | bytes 196616 | tf_op jit(solution)/shard_map/ppermute | solution.py:113
  11.6 10.5 %collective-permute-start.4 = (bf16[1,16,4,512]{3,2,1,0:T(4,128)(2,1)S(1)}, bf16[1,16,4,512]{3,2,1,0:T(4,128)(2,1)S(1)}, u32[]{:S(2)}, u32[]{:S(2)}) collective-permute-start(bf16[1,16,4,512]{3,2,1,0:T(4,128)(2,1)S(1)} %get-tuple-element.12), channel_id=1, source_target_pairs={{0,5},{1,4},{2,7},{3,6},{4,1},{5,0},{6,3},{7,2},{8,13},{9,12},{10,... | collective-permute-start | bytes 196616 | tf_op jit(solution)/shard_map/ppermute | solution.py:113
  11.9 17.6 %copy-start.5 = (s32[3]{0:T(128)S(1)}, s32[3]{0:T(128)}, u32[]{:S(2)}) copy-start(s32[3]{0:T(128)} %param.7) | copy-start | bytes 40
  11.9 21.4 %copy-start.7 = (s32[4]{0:T(128)S(1)}, s32[4]{0:T(128)}, u32[]{:S(2)}) copy-start(s32[4]{0:T(128)} %constant.256.clone) | copy-start | bytes 52
  12.1 10.1 %collective-permute-start.5 = (bf16[1,16,4,512]{3,2,1,0:T(4,128)(2,1)S(1)}, bf16[1,16,4,512]{3,2,1,0:T(4,128)(2,1)S(1)}, u32[]{:S(2)}, u32[]{:S(2)}) collective-permute-start(bf16[1,16,4,512]{3,2,1,0:T(4,128)(2,1)S(1)} %get-tuple-element.11), channel_id=1, source_target_pairs={{0,6},{1,7},{2,4},{3,5},{4,2},{5,3},{6,0},{7,1},{8,14},{9,15},{10,... | collective-permute-start | bytes 196616 | tf_op jit(solution)/shard_map/ppermute | solution.py:113
  15.7 6.6 %collective-permute-start.6 = (bf16[1,16,4,512]{3,2,1,0:T(4,128)(2,1)S(1)}, bf16[1,16,4,512]{3,2,1,0:T(4,128)(2,1)S(1)}, u32[]{:S(2)}, u32[]{:S(2)}) collective-permute-start(bf16[1,16,4,512]{3,2,1,0:T(4,128)(2,1)S(1)} %get-tuple-element.10), channel_id=1, source_target_pairs={{0,7},{1,6},{2,5},{3,4},{4,3},{5,2},{6,1},{7,0},{8,15},{9,14},{10,... | collective-permute-start | bytes 196616 | tf_op jit(solution)/shard_map/ppermute | solution.py:113
  22.4 11.0 %collective-permute-start.8 = (bf16[4,32,512]{2,1,0:T(8,128)(2,1)S(1)}, bf16[4,32,512]{2,1,0:T(8,128)(2,1)S(1)}, u32[]{:S(2)}, u32[]{:S(2)}) collective-permute-start(bf16[4,32,512]{2,1,0:T(8,128)(2,1)S(1)} %get-tuple-element.9), channel_id=1, source_target_pairs={{1,0},{2,1},{3,2},{4,3},{5,4},{6,5},{7,6},{9,8},{10,9},{11,10},{12... | collective-permute-start | bytes 393224 | tf_op jit(solution)/shard_map/ppermute | solution.py:21
  24.7 8.7 %collective-permute-start.7 = (bf16[4,32,512]{2,1,0:T(8,128)(2,1)S(1)}, bf16[4,32,512]{2,1,0:T(8,128)(2,1)S(1)}, u32[]{:S(2)}, u32[]{:S(2)}) collective-permute-start(bf16[4,32,512]{2,1,0:T(8,128)(2,1)S(1)} %get-tuple-element.8), channel_id=1, source_target_pairs={{0,1},{1,2},{2,3},{3,4},{4,5},{5,6},{6,7},{8,9},{9,10},{10,11},{11... | collective-permute-start | bytes 393224 | tf_op jit(solution)/shard_map/ppermute | solution.py:18
  33.7 19.9 %collective-permute-start.9 = (bf16[24,32,6]{2,1,0:T(8,128)(2,1)S(1)}, bf16[24,32,6]{2,1,0:T(8,128)(2,1)S(1)}, u32[]{:S(2)}, u32[]{:S(2)}) collective-permute-start(bf16[24,32,6]{2,1,0:T(8,128)(2,1)S(1)} %get-tuple-element.7), channel_id=1, source_target_pairs={{0,8},{8,16},{16,24},{1,9},{9,17},{17,25},{2,10},{10,18},{18,26},{... | collective-permute-start | bytes 27656 | tf_op jit(solution)/shard_map/ppermute | solution.py:29
  36.8 12.4 %collective-permute-start.10 = (bf16[24,32,6]{2,1,0:T(8,128)(2,1)S(1)}, bf16[24,32,6]{2,1,0:T(8,128)(2,1)S(1)}, u32[]{:S(2)}, u32[]{:S(2)}) collective-permute-start(bf16[24,32,6]{2,1,0:T(8,128)(2,1)S(1)} %get-tuple-element.6), channel_id=1, source_target_pairs={{8,0},{16,8},{24,16},{9,1},{17,9},{25,17},{10,2},{18,10},{26,18},{... | collective-permute-start | bytes 27656 | tf_op jit(solution)/shard_map/ppermute | solution.py:29
  53.6 0.7 copy-start
  119.6 0.8 copy-start.6
  119.7 6.7 %copy-start.1 = (bf16[24,32,6]{2,1,0:T(8,128)(2,1)S(1)}, bf16[24,32,6]{2,1,0:T(8,128)(2,1)}, u32[]{:S(2)}) copy-start(bf16[24,32,6]{2,1,0:T(8,128)(2,1)} %copy-done) | copy-start | bytes 27652
  120.0 7.1 %copy-start.4 = (bf16[8,16,256]{2,1,0:T(8,128)(2,1)}, bf16[8,16,256]{2,1,0:T(8,128)(2,1)S(1)}, u32[]{:S(2)}) copy-start(bf16[8,16,256]{2,1,0:T(8,128)(2,1)S(1)} %copy.28) | copy-start | bytes 196612
  120.7 16.0 %collective-permute-start.12 = (f32[2,16,128]{2,1,0:T(8,128)S(1)}, f32[2,16,128]{2,1,0:T(8,128)S(1)}, u32[]{:S(2)}, u32[]{:S(2)}) collective-permute-start(f32[2,16,128]{2,1,0:T(8,128)S(1)} %get-tuple-element.18), channel_id=1, source_target_pairs={{1,0},{2,1},{3,2},{4,3},{5,4},{6,5},{7,6},{9,8},{10,9},{11,10},{12... | collective-permute-start | bytes 49160 | tf_op jit(solution)/shard_map/ppermute | solution.py:21
  122.7 14.0 %collective-permute-start.11 = (f32[2,16,128]{2,1,0:T(8,128)S(1)}, f32[2,16,128]{2,1,0:T(8,128)S(1)}, u32[]{:S(2)}, u32[]{:S(2)}) collective-permute-start(f32[2,16,128]{2,1,0:T(8,128)S(1)} %get-tuple-element.17), channel_id=1, source_target_pairs={{0,1},{1,2},{2,3},{3,4},{4,5},{5,6},{6,7},{8,9},{9,10},{10,11},{11... | collective-permute-start | bytes 49160 | tf_op jit(solution)/shard_map/ppermute | solution.py:18
  127.2 1.4 %copy-start.3 = (f32[24,32,512]{2,1,0:T(8,128)S(1)}, f32[24,32,512]{2,1,0:T(8,128)}, u32[]{:S(2)}) copy-start(f32[24,32,512]{2,1,0:T(8,128)} %fusion.50) | copy-start | bytes 4718596
  128.6 1.4 %copy-start.2 = (f32[24,32,512]{2,1,0:T(8,128)S(1)}, f32[24,32,512]{2,1,0:T(8,128)}, u32[]{:S(2)}) copy-start(f32[24,32,512]{2,1,0:T(8,128)} %fusion.52) | copy-start | bytes 4718596
